TPU v7x, 32 devices: a whole 2x2x4 slice. The times are simulated.
32 devices in a mesh: ens: 2 (over y), grid: 4 (over z), pole: 4 (over x, core).
Axes of the slice: x: 2, y: 2, z: 4, core: 2. Of those that a mesh axis runs over, the one named last changes fastest.
Arguments:
- inverse_pool: bfloat16 [8, 2, 4096, 4096], P(('ens', 'pole'), None, 'grid'), parts along dimension 0, may hold values from -6 to 6
- factor_tiles: bfloat16 [8, 4, 2, 10, 256, 256], P(('ens', 'pole'), None, None, None, 'grid'), parts along dimension 0, may hold values from -0.078125 to 0.078125
- diag_inverse: bfloat16 [8, 2, 1024, 256], P(('ens', 'pole'), None, 'grid'), parts along dimension 0, may hold values from -6 to 6
- pole_weight: float32 [4, 2], P('pole'), may hold values from -3 to 3
- ancestors: int32 [4, 10], replicated, may hold values from 0 to 15, all different within a row
Outputs:
- density_panel: float32 [8192, 1024], P(('ens', 'grid'), 'pole'), parts along dimension 0
- density_diagonal: float32 [2048, 256], P(('ens', 'grid')), parts along dimension 0
There are 2 independent parts, one for each index of `ens`. A program takes and returns all parts, laid end to end along the dimension named above; an argument that names none is the same for every part. Nothing has to cross between parts.
Inputs may be any that keep to these rules, and one draw needn't show every extreme that they name: `ancestors`: each row names 10 different ancestor blocks; every one of the 16 blocks is named by some row.
All inputs are finite; a program needn't handle non-finite values.
Results may differ from a plain program's by a relative error of at most 0.0022.
Values may be sent and summed in bfloat16 or wider, within the bound.
A program may use at most 128 MiB of HBM per device.

v0:
```python
import functools

import jax
import jax.numpy as jnp
from jax import lax
from jax.experimental import pallas as pl
from jax.experimental.pallas import tpu as pltpu
from jax.sharding import PartitionSpec as P

MESH = pl.DeviceIdType.MESH
HALVES = 2


def plain_product(left, right):
    return jnp.dot(left, right, preferred_element_type=jnp.float32)


def turned_product(left, right):
    return lax.dot_general(
        left, right, (((0,), (0,)), ((), ())), preferred_element_type=jnp.float32
    )


def portion_terms(rows_pair, block_index, offset, listed, factors, weights):
    tile_width = factors.shape[3]
    listed_count = factors.shape[1]
    height = rows_pair.shape[1]
    blocks = rows_pair.shape[2] // tile_width
    matches = listed == block_index

    def compute():
        chosen = rows_pair.reshape(2, height, blocks, tile_width)[:, :, listed, :].reshape(
            2, height, listed_count * tile_width
        )
        stacked = factors.reshape(2, listed_count * tile_width, tile_width)
        part_real = -(plain_product(chosen[0], stacked[0]) - plain_product(chosen[1], stacked[1]))
        part_imag = -(plain_product(chosen[0], stacked[1]) + plain_product(chosen[1], stacked[0]))
        panel_piece = weights[0] * part_imag + weights[1] * part_real
        rounded_real = part_real.astype(jnp.bfloat16)
        rounded_imag = part_imag.astype(jnp.bfloat16)
        position = jnp.sum(jnp.where(matches, jnp.arange(listed_count, dtype=jnp.int32), 0))
        matched = lax.dynamic_slice(
            factors, (jnp.int32(0), position, offset, jnp.int32(0)), (2, 1, height, tile_width)
        )[:, 0]
        diag_real = -(
            turned_product(matched[0], rounded_real) - turned_product(matched[1], rounded_imag)
        )
        diag_imag = -(
            turned_product(matched[0], rounded_imag) + turned_product(matched[1], rounded_real)
        )
        return (panel_piece, weights[0] * diag_imag + weights[1] * diag_real)

    def skipped():
        return (
            jnp.zeros((height, tile_width), jnp.float32),
            jnp.zeros((tile_width, tile_width), jnp.float32),
        )

    return lax.cond(jnp.any(matches), compute, skipped)


def rows_terms(rows_pair, row_first, listed, factors, weights):
    tile_width = factors.shape[3]
    height = rows_pair.shape[1]
    piece_rows = min(height, tile_width)
    panels = []
    diag_total = jnp.zeros((tile_width, tile_width), jnp.float32)
    for portion in range(height // piece_rows):
        row_start = row_first + portion * piece_rows
        panel_piece, diag_piece = portion_terms(
            rows_pair[:, portion * piece_rows : (portion + 1) * piece_rows],
            row_start // tile_width,
            row_start % tile_width,
            listed,
            factors,
            weights,
        )
        panels.append(panel_piece)
        diag_total = diag_total + diag_piece
    return (jnp.concatenate(panels, axis=0), diag_total)


def shards(inverse_pool, factor_tiles, diag_inverse, pole_weight, ancestors):
    device_index = lax.axis_index("grid")
    rows_here = inverse_pool.shape[2]
    supers = factor_tiles.shape[1]
    tile_width = factor_tiles.shape[5]
    row_slab = inverse_pool[0]
    weights = (pole_weight[0, 0], pole_weight[0, 1])
    row_first = device_index * rows_here
    own_panels = []
    diag_terms = []
    for supernode in range(supers):
        factors = lax.all_gather(factor_tiles[0, supernode], "grid", axis=2, tiled=True)
        listed = ancestors[supernode]
        own_panel, own_diag = rows_terms(row_slab, row_first, listed, factors, weights)
        diag_terms.append(own_diag)
        own_panels.append(own_panel)
    panel_rows = jnp.concatenate(own_panels, axis=1)
    panel_share = lax.psum_scatter(panel_rows, "pole", scatter_dimension=1, tiled=True)
    diag_term = jnp.stack(diag_terms, axis=0).reshape(supers * tile_width, tile_width)
    diag_local = diag_inverse[0]
    local_block = weights[0] * diag_local[1].astype(jnp.float32) + weights[1] * diag_local[
        0
    ].astype(jnp.float32)
    share_rows = local_block.shape[0]
    placed = lax.dynamic_update_slice(
        jnp.zeros_like(diag_term), local_block, (device_index * share_rows, jnp.int32(0))
    )
    spread = lax.psum_scatter(diag_term + placed, ("grid", "pole"), scatter_dimension=0, tiled=True)
    diag_share = lax.all_gather(spread, "pole", axis=0, tiled=True)
    return (panel_share, diag_share)


def fused_kernel(
    grid_size, pole_size, ancestors, weight, pool, tiles, diag_in,
    panel_out, diag_out,
    rows, sent_panel, got_panel, column, own_diag, sent_diag, diag_local, pole_sums, grid_send, grid_sums, final,
    pool_sem, tile_sem, diag_sem, up_sem, down_sem, arrive_sem,
    panel_send, panel_recv, a_send, a_recv, b_send, b_recv, c_send, c_recv, *factors,
):
    g = lax.axis_index("grid")
    q = lax.axis_index("pole")
    supers, listed_count = ancestors.shape
    half = factors[0].shape[3] // 2
    width = factors[0].shape[2]
    slice_rows = width // grid_size
    share = width // pole_size
    blocks = rows.shape[2] // width
    chunks = [(k, c) for k in range(supers) for c in range(HALVES)]

    tile_copies = []
    for j, (k, c) in enumerate(chunks):
        for part in range(2):
            copy = pltpu.make_async_copy(
                tiles.at[0, k, part, :, :, pl.ds(c * half, half)],
                factors[k].at[c, :, pl.ds(g * slice_rows, slice_rows), pl.ds(part * half, half)],
                tile_sem.at[j, part],
            )
            copy.start()
            tile_copies.append(copy)
    diag_copy = pltpu.make_async_copy(diag_in.at[0], diag_local, diag_sem)
    diag_copy.start()

    barrier = pltpu.get_barrier_semaphore()
    for step in range(1, grid_size):
        pl.semaphore_signal(
            barrier, inc=1, device_id={"grid": lax.rem(g + step, grid_size)}, device_id_type=MESH
        )
    for step in range(1, pole_size):
        pl.semaphore_signal(
            barrier, inc=1, device_id={"pole": lax.rem(q + step, pole_size)}, device_id_type=MESH
        )
    pl.semaphore_wait(barrier, grid_size - 1 + pole_size - 1)

    def piece(j, source):
        k, c = chunks[j]
        return factors[k].at[c, :, pl.ds(source * slice_rows, slice_rows), :]

    def hop(j, source, up):
        return pltpu.make_async_remote_copy(
            src_ref=piece(j, source),
            dst_ref=piece(j, source),
            send_sem=(up_sem if up else down_sem).at[j, source],
            recv_sem=arrive_sem.at[j, source],
            device_id={"grid": g + 1 if up else g - 1},
            device_id_type=MESH,
        )

    def pass_on(j, distance):
        low = g - distance
        high = g + distance
        if distance:
            @pl.when(low >= 0)
            def _():
                hop(j, low, True).wait_recv()

        @pl.when(jnp.logical_and(low >= 0, g + 1 < grid_size))
        def _():
            hop(j, low, True).start()

        if distance:
            @pl.when(high < grid_size)
            def _():
                hop(j, high, False).wait_recv()

        @pl.when(jnp.logical_and(high < grid_size, g >= 1))
        def _():
            hop(j, high, False).start()

    for j in range(len(chunks)):
        tile_copies[2 * j].wait()
        tile_copies[2 * j + 1].wait()
        pass_on(j, 0)
    pool_copies = []
    for part in range(2):
        for a in range(rows.shape[1]):
            copy = pltpu.make_async_copy(
                pool.at[0, part, :, pl.ds(a * width, width)], rows.at[part, a], pool_sem.at[part, a]
            )
            copy.start()
            pool_copies.append(copy)
    for distance in range(1, grid_size - 1):
        for j in range(len(chunks)):
            pass_on(j, distance)
    for copy in pool_copies:
        copy.wait()
    diag_copy.wait()

    w_real = weight[0, 0]
    w_imag = weight[0, 1]

    def panel_copy(j, k, c, b):
        slot = lax.rem(q - k + pole_size, pole_size) - 1
        span = pl.ds(b * width, width)
        return pltpu.make_async_remote_copy(
            src_ref=sent_panel.at[k, c, span],
            dst_ref=got_panel.at[slot, c, span],
            send_sem=panel_send.at[j, b],
            recv_sem=panel_recv.at[slot, c, b],
            device_id={"pole": k},
            device_id_type=MESH,
        )

    def share_copy(k, r):
        return pltpu.make_async_remote_copy(
            src_ref=sent_diag.at[k, pl.ds(r * share, share)],
            dst_ref=pole_sums.at[k, q],
            send_sem=a_send.at[k, r],
            recv_sem=a_recv.at[k, q],
            device_id={"pole": r},
            device_id_type=MESH,
        )

    def place_of(k, block):
        count = jnp.int32(0)
        position = jnp.int32(0)
        for n in range(listed_count):
            hit = (ancestors[k, n] == block).astype(jnp.int32)
            count = count + hit
            position = position + hit * n
        return count, jnp.clip(position, 0, listed_count - 1)

    def grid_copy(k):
        return pltpu.make_async_remote_copy(
            src_ref=grid_send.at[k],
            dst_ref=grid_sums.at[g],
            send_sem=b_send.at[k],
            recv_sem=b_recv.at[g],
            device_id={"grid": k},
            device_id_type=MESH,
        )

    def final_copy(r):
        mine = pl.ds(pl.multiple_of(q * share, share), share)
        return pltpu.make_async_remote_copy(
            src_ref=final.at[mine],
            dst_ref=final.at[mine],
            send_sem=c_send.at[r],
            recv_sem=c_recv.at[q],
            device_id={"pole": r},
            device_id_type=MESH,
        )

    def landing(buffer, semaphore):
        return pltpu.make_async_remote_copy(
            src_ref=buffer, dst_ref=buffer, send_sem=semaphore, recv_sem=semaphore,
            device_id={"pole": q}, device_id_type=MESH,
        )

    def to_owner(k):
        for r in range(pole_size):
            @pl.when(q != r)
            def _():
                landing(pole_sums.at[k, r], a_recv.at[k, r]).wait_recv()
        summed = own_diag[k, pl.ds(pl.multiple_of(q * share, share), share), :]
        for step in range(1, pole_size):
            summed = summed + pole_sums[k, lax.rem(q + step, pole_size)].astype(jnp.float32)
        grid_send[k] = summed

        @pl.when(g != k)
        def _():
            grid_copy(k).start()

        @pl.when(g == k)
        def _():
            grid_sums[g] = grid_send[k]

    for j, (k, c) in enumerate(chunks):
        pass_on(j, grid_size - 1)

        @pl.loop(0, blocks)
        def _(b):
            span = pl.ds(pl.multiple_of(b * width, width), width)
            with_real = jnp.zeros((width, 2 * half), jnp.float32)
            with_imag = jnp.zeros((width, 2 * half), jnp.float32)
            for n in range(listed_count):
                source = jnp.clip(ancestors[k, n], 0, rows.shape[1] - 1)
                factor = factors[k][c, n]
                with_real += jnp.dot(
                    rows[0, source, span, :], factor, preferred_element_type=jnp.float32
                )
                with_imag += jnp.dot(
                    rows[1, source, span, :], factor, preferred_element_type=jnp.float32
                )
            count, _ = place_of(k, g * blocks + b)
            keep = jnp.full((width, half), count, jnp.int32) > 0
            real = jnp.where(keep, with_imag[:, half:] - with_real[:, :half], 0.0)
            imag = jnp.where(keep, -(with_real[:, half:] + with_imag[:, :half]), 0.0)
            column[span, pl.ds(c * 2 * half, half)] = real.astype(jnp.bfloat16)
            column[span, pl.ds(c * 2 * half + half, half)] = imag.astype(jnp.bfloat16)
            term = w_real * imag + w_imag * real
            sent_panel[k, c, span, :] = term.astype(jnp.bfloat16)

            @pl.when(q == k)
            def _():
                panel_out[span, pl.ds(c * half, half)] = term

            @pl.when(q != k)
            def _():
                panel_copy(j, k, c, b).start()

        if c == HALVES - 1:
            for left in range(HALVES):
                for right in range(HALVES):
                    def add(b, total):
                        _, position = place_of(k, g * blocks + b)
                        span = pl.ds(pl.multiple_of(b * width, width), width)
                        return total + lax.dot_general(
                            factors[k][left, position],
                            column[span, pl.ds(right * 2 * half, 2 * half)],
                            (((0,), (0,)), ((), ())),
                            preferred_element_type=jnp.float32,
                        )

                    total = jnp.zeros((2 * half, 2 * half), jnp.float32)
                    for b in range(blocks):
                        total = add(b, total)
                    real = total[half:, half:] - total[:half, :half]
                    imag = -(total[:half, half:] + total[half:, :half])
                    own_diag[k, pl.ds(left * half, half), pl.ds(right * half, half)] = (
                        w_real * imag + w_imag * real
                    )

            @pl.when(g == k)
            def _():
                own_diag[k] = (
                    own_diag[k]
                    + w_real * diag_local[1].astype(jnp.float32)
                    + w_imag * diag_local[0].astype(jnp.float32)
                )

            sent_diag[k] = own_diag[k].astype(jnp.bfloat16)
            for r in range(pole_size):
                @pl.when(q != r)
                def _():
                    share_copy(k, r).start()

            if k:
                to_owner(k - 1)

    to_owner(supers - 1)
    for s in range(grid_size):
        @pl.when(g != s)
        def _():
            landing(grid_sums.at[s], b_recv.at[s]).wait_recv()
    summed = grid_sums[0]
    for s in range(1, grid_size):
        summed = summed + grid_sums[s]
    final[pl.ds(pl.multiple_of(q * share, share), share), :] = summed
    for r in range(pole_size):
        @pl.when(q != r)
        def _():
            final_copy(r).start()

    for c in range(HALVES):
        @pl.loop(0, blocks)
        def _(b):
            span = pl.ds(pl.multiple_of(b * width, width), width)
            for slot in range(pole_size - 1):
                landing(got_panel.at[slot, c, span], panel_recv.at[slot, c, b]).wait_recv()
            lanes = pl.ds(c * half, half)
            total = panel_out[span, lanes]
            for slot in range(pole_size - 1):
                total = total + got_panel[slot, c, span, :].astype(jnp.float32)
            panel_out[span, lanes] = total

    for r in range(pole_size):
        @pl.when(q != r)
        def _():
            landing(final.at[pl.ds(r * share, share)], c_recv.at[r]).wait_recv()
    diag_out[...] = final[...]

    for distance in range(grid_size - 1):
        for j in range(len(chunks)):
            @pl.when(jnp.logical_and(g - distance >= 0, g + 1 < grid_size))
            def _():
                hop(j, g - distance, True).wait_send()

            @pl.when(jnp.logical_and(g + distance < grid_size, g >= 1))
            def _():
                hop(j, g + distance, False).wait_send()
    for j, (k, c) in enumerate(chunks):
        for b in range(blocks):
            @pl.when(q != k)
            def _():
                panel_copy(j, k, c, b).wait_send()
    for k in range(supers):
        for r in range(pole_size):
            @pl.when(q != r)
            def _():
                share_copy(k, r).wait_send()

        @pl.when(g != k)
        def _():
            grid_copy(k).wait_send()
    for r in range(pole_size):
        @pl.when(q != r)
        def _():
            final_copy(r).wait_send()


def fused(grid_size, pole_size, inverse_pool, factor_tiles, diag_inverse, pole_weight, ancestors):
    supers, listed_count = ancestors.shape
    width = factor_tiles.shape[5]
    height = inverse_pool.shape[2]
    half = width // HALVES
    share = width // pole_size
    chunks = supers * HALVES
    blocks = height // width
    dma = pltpu.SemaphoreType.DMA
    f32 = jnp.float32
    bf16 = jnp.bfloat16
    scratch = [
        pltpu.VMEM((2, inverse_pool.shape[3] // width, height, width), bf16),
        pltpu.VMEM((supers, HALVES, height, half), bf16),
        pltpu.VMEM((pole_size - 1, HALVES, height, half), bf16),
        pltpu.VMEM((height, 2 * width), bf16),
        pltpu.VMEM((supers, width, width), f32),
        pltpu.VMEM((supers, width, width), bf16),
        pltpu.VMEM(diag_inverse.shape[1:], bf16),
        pltpu.VMEM((supers, pole_size, share, width), bf16),
        pltpu.VMEM((supers, share, width), f32),
        pltpu.VMEM((grid_size, share, width), f32),
        pltpu.VMEM((width, width), f32),
        dma((2, inverse_pool.shape[3] // width)), dma((chunks, 2)), dma(()),
        dma((chunks, grid_size)), dma((chunks, grid_size)), dma((chunks, grid_size)),
        dma((chunks, blocks)), dma((pole_size - 1, HALVES, blocks)),
        dma((supers, pole_size)), dma((supers, pole_size)),
        dma((supers,)), dma((grid_size,)),
        dma((pole_size,)), dma((pole_size,)),
    ] + [pltpu.VMEM((HALVES, listed_count, width, 2 * half), bf16)] * supers
    smem = pl.BlockSpec(memory_space=pltpu.SMEM)
    vmem = pl.BlockSpec(memory_space=pltpu.VMEM)
    anywhere = pl.BlockSpec(memory_space=pl.ANY)
    return pl.pallas_call(
        functools.partial(fused_kernel, grid_size, pole_size),
        out_shape=(
            jax.ShapeDtypeStruct((height, width), f32),
            jax.ShapeDtypeStruct((width, width), f32),
        ),
        in_specs=[smem, smem, anywhere, anywhere, anywhere],
        out_specs=(vmem, vmem),
        scratch_shapes=scratch,
        compiler_params=pltpu.CompilerParams(
            collective_id=0, has_side_effects=True, vmem_limit_bytes=56 * 2**20
        ),
    )(ancestors, pole_weight, inverse_pool, factor_tiles, diag_inverse)


def choose(grid_size, pole_size, inverse_pool, factor_tiles, diag_inverse, pole_weight, ancestors):
    supers = ancestors.shape[0]
    width = factor_tiles.shape[5]
    whole_blocks = inverse_pool.shape[2] % width == 0 and factor_tiles.shape[4] % 16 == 0
    if whole_blocks and supers == grid_size == pole_size and width % (HALVES * 128) == 0:
        return fused(
            grid_size, pole_size, inverse_pool, factor_tiles, diag_inverse, pole_weight, ancestors
        )
    return shards(inverse_pool, factor_tiles, diag_inverse, pole_weight, ancestors)


def solution(mesh):
    in_specs = (
        P(("ens", "pole"), None, "grid", None),
        P(("ens", "pole"), None, None, None, "grid", None),
        P(("ens", "pole"), None, "grid", None),
        P("pole", None),
        P(),
    )
    out_specs = (P(("ens", "grid"), "pole"), P(("ens", "grid"), None))
    body = functools.partial(choose, mesh.shape["grid"], mesh.shape["pole"])
    return jax.shard_map(body, mesh=mesh, in_specs=in_specs, out_specs=out_specs, check_vma=False)
```

profile of v0, /device:TPU:29, one launch (start us, length us, event | category | flops | bytes accessed | tf_op | source)
XLA Modules:
  0.0 200.4 jit_solution(11761488176701533107)
XLA Ops:
  0.6 195.8 %shard_map.68 = (f32[1024,256]{1,0:T(8,128)}, f32[256,256]{1,0:T(8,128)}) custom-call(s32[4,10]{1,0:T(4,128)} %ancestors.1, f32[1,2]{1,0:T(1,128)} %weight.1, bf16[1,2,1024,4096]{3,2,1,0:T(8,128)(2,1)} %pool.1, bf16[1,4,2,10,64,256]{5,4,3,2,1,0:T(8,128)(2,1)} %tiles.1, bf16[1,2,256,256]{3,2,1,0:T(8,128)(2,1)} %diag_in.1), custom_call_target="tpu_custom_call" | custom-call | tf_op jit(solution)/shard_map/pallas_call | solution.py:456
  196.4 2.3 %copy.9 = f32[1024,256]{1,0:T(8,128)} copy(f32[1024,256]{1,0:T(8,128)} %get-tuple-element.4) | data formatting | bytes 2097152
  198.7 1.7 copy.10
where the time goes:
time: 201 us; the launch traced here: 200 us
  Pallas kernels  196 us (98%)
  local copies, waits for them, and re-layouts  3.93 us (2%)
    pallas_call x1, Pallas kernels, fused(): pl.pallas_call(functools.partial(fused_kernel, grid_size, pole_size), out...  196 us

commit v1 on v0

--- a/solution.py
+++ b/solution.py
@@ -9,6 +9,7 @@
 
 MESH = pl.DeviceIdType.MESH
 HALVES = 2
+AHEAD = 2
 
 
 def plain_product(left, right):
@@ -188,10 +189,13 @@
         def _():
             hop(j, high, False).start()
 
-    for j in range(len(chunks)):
+    def own(j):
         tile_copies[2 * j].wait()
         tile_copies[2 * j + 1].wait()
         pass_on(j, 0)
+
+    for j in range(min(AHEAD, len(chunks))):
+        own(j)
     pool_copies = []
     for part in range(2):
         for a in range(rows.shape[1]):
@@ -200,9 +204,14 @@
             )
             copy.start()
             pool_copies.append(copy)
-    for distance in range(1, grid_size - 1):
-        for j in range(len(chunks)):
+
+    def bring(j):
+        if j + AHEAD < len(chunks):
+            own(j + AHEAD)
+        for distance in range(1, grid_size - 1):
             pass_on(j, distance)
+
+    bring(0)
     for copy in pool_copies:
         copy.wait()
     diag_copy.wait()
@@ -287,6 +296,8 @@
             grid_sums[g] = grid_send[k]
 
     for j, (k, c) in enumerate(chunks):
+        if j:
+            bring(j)
         pass_on(j, grid_size - 1)
 
         @pl.loop(0, blocks)

time: 201 us -> 204 us (1.015)
  the two profiles are of different devices: /device:TPU:29 before, /device:TPU:25 now
where the time goes in v1:
time: 204 us
  Pallas kernels  200 us (98%)
  local copies, waits for them, and re-layouts  3.93 us (2%)
    pallas_call x1, Pallas kernels, fused(): pl.pallas_call(functools.partial(fused_kernel, grid_size, pole_size), out...  200 us

profile of v1, /device:TPU:25, one launch (start us, length us, event | category | flops | bytes accessed | tf_op | source)
XLA Modules:
  0.0 204.1 jit_solution(17455417745291649880)
XLA Ops:
  0.6 199.5 %shard_map.68 = (f32[1024,256]{1,0:T(8,128)}, f32[256,256]{1,0:T(8,128)}) custom-call(s32[4,10]{1,0:T(4,128)} %ancestors.1, f32[1,2]{1,0:T(1,128)} %weight.1, bf16[1,2,1024,4096]{3,2,1,0:T(8,128)(2,1)} %pool.1, bf16[1,4,2,10,64,256]{5,4,3,2,1,0:T(8,128)(2,1)} %tiles.1, bf16[1,2,256,256]{3,2,1,0:T(8,128)(2,1)} %diag_in.1), custom_call_target="tpu_custom_call" | custom-call | tf_op jit(solution)/shard_map/pallas_call | solution.py:467
  200.1 2.3 %copy.9 = f32[1024,256]{1,0:T(8,128)} copy(f32[1024,256]{1,0:T(8,128)} %get-tuple-element.4) | data formatting | bytes 2097152
  202.4 1.7 copy.10

commit v2 on v0

--- a/solution.py
+++ b/solution.py
@@ -9,6 +9,12 @@
 
 MESH = pl.DeviceIdType.MESH
 HALVES = 2
+AHEAD = 2
+SHIFTED = 48
+LANES = 128
+GROUP = 8
+AID_STEPS = (3, 5, 7, 8)
+RETURN_STEPS = (4, 6, 8, 8)
 
 
 def plain_product(left, right):
@@ -116,25 +122,35 @@
     grid_size, pole_size, ancestors, weight, pool, tiles, diag_in,
     panel_out, diag_out,
     rows, sent_panel, got_panel, column, own_diag, sent_diag, diag_local, pole_sums, grid_send, grid_sums, final,
-    pool_sem, tile_sem, diag_sem, up_sem, down_sem, arrive_sem,
-    panel_send, panel_recv, a_send, a_recv, b_send, b_recv, c_send, c_recv, *factors,
+    select, packed, shifted_tiles, spread, aid_column, aid_sent, aid_got, aid_own, returned, column_rows,
+    pool_sem, tile_sem, diag_sem, shifted_sem, up_sem, down_sem, arrive_sem,
+    panel_send, panel_recv, a_send, a_recv, b_send, b_recv, c_send, c_recv,
+    packed_send, packed_recv, aid_send, aid_recv, return_send, return_recv, rows_send, rows_recv, *factors,
 ):
     g = lax.axis_index("grid")
     q = lax.axis_index("pole")
     supers, listed_count = ancestors.shape
-    half = factors[0].shape[3] // 2
-    width = factors[0].shape[2]
+    last = grid_size - 1
+    half = factors[0].shape[2] // 2
+    width = factors[0].shape[1]
     slice_rows = width // grid_size
     share = width // pole_size
+    total_blocks = rows.shape[1]
     blocks = rows.shape[2] // width
-    chunks = [(k, c) for k in range(supers) for c in range(HALVES)]
+    order = [0, 3, 2, 1]
+    chunks = [(k, c) for k in order for c in range(HALVES)]
+    count = len(chunks)
+    is_end = jnp.logical_or(g == 0, g == last)
+    is_mid = jnp.logical_not(is_end)
+    partner = jnp.where(g < 2, 1 - g, 5 - g)
+    shift_first = pl.multiple_of(slice_rows * jnp.where(is_end, partner, g), 16)
 
     tile_copies = []
     for j, (k, c) in enumerate(chunks):
         for part in range(2):
             copy = pltpu.make_async_copy(
                 tiles.at[0, k, part, :, :, pl.ds(c * half, half)],
-                factors[k].at[c, :, pl.ds(g * slice_rows, slice_rows), pl.ds(part * half, half)],
+                factors[j].at[:, pl.ds(g * slice_rows, slice_rows), pl.ds(part * half, half)],
                 tile_sem.at[j, part],
             )
             copy.start()
@@ -142,6 +158,23 @@
     diag_copy = pltpu.make_async_copy(diag_in.at[0], diag_local, diag_sem)
     diag_copy.start()
 
+    def shifted_copies():
+        return [
+            pltpu.make_async_copy(
+                tiles.at[0, k, part, :, pl.ds(0, SHIFTED), pl.ds(c * half, half)],
+                shifted_tiles.at[k * HALVES + c, :, :, pl.ds(part * half, half)],
+                shifted_sem.at[k, c, part],
+            )
+            for k in range(supers)
+            for c in range(HALVES)
+            for part in range(2)
+        ]
+
+    @pl.when(is_mid)
+    def _():
+        for copy in shifted_copies():
+            copy.start()
+
     barrier = pltpu.get_barrier_semaphore()
     for step in range(1, grid_size):
         pl.semaphore_signal(
@@ -153,59 +186,173 @@
         )
     pl.semaphore_wait(barrier, grid_size - 1 + pole_size - 1)
 
-    def piece(j, source):
-        k, c = chunks[j]
-        return factors[k].at[c, :, pl.ds(source * slice_rows, slice_rows), :]
-
-    def hop(j, source, up):
-        return pltpu.make_async_remote_copy(
-            src_ref=piece(j, source),
-            dst_ref=piece(j, source),
+    def hop(j, source, up, trimmed=False):
+        first = source * slice_rows + (SHIFTED if trimmed else 0)
+        size = slice_rows - (SHIFTED if trimmed else 0)
+        piece = factors[j].at[:, pl.ds(pl.multiple_of(first, 16), size), :]
+        return pltpu.make_async_remote_copy(
+            src_ref=piece,
+            dst_ref=piece,
             send_sem=(up_sem if up else down_sem).at[j, source],
             recv_sem=arrive_sem.at[j, source],
             device_id={"grid": g + 1 if up else g - 1},
             device_id_type=MESH,
         )
 
-    def pass_on(j, distance):
-        low = g - distance
-        high = g + distance
-        if distance:
-            @pl.when(low >= 0)
-            def _():
-                hop(j, low, True).wait_recv()
-
-        @pl.when(jnp.logical_and(low >= 0, g + 1 < grid_size))
-        def _():
-            hop(j, low, True).start()
-
-        if distance:
-            @pl.when(high < grid_size)
-            def _():
-                hop(j, high, False).wait_recv()
-
-        @pl.when(jnp.logical_and(high < grid_size, g >= 1))
-        def _():
-            hop(j, high, False).start()
-
-    for j in range(len(chunks)):
-        tile_copies[2 * j].wait()
-        tile_copies[2 * j + 1].wait()
-        pass_on(j, 0)
+    def own_full(j, who):
+        @pl.when(jnp.logical_and(who, g <= 1))
+        def _():
+            hop(j, g, True).start()
+
+        @pl.when(jnp.logical_and(who, g >= 2))
+        def _():
+            hop(j, g, False).start()
+
+    def own_trimmed(j):
+        @pl.when(g == 2)
+        def _():
+            hop(j, g, True, True).start()
+
+        @pl.when(g == 1)
+        def _():
+            hop(j, g, False, True).start()
+
+    def packed_copy(p):
+        i, part = divmod(p, 2)
+        return pltpu.make_async_remote_copy(
+            src_ref=packed.at[part, i],
+            dst_ref=packed.at[part, i],
+            send_sem=packed_send.at[part, i],
+            recv_sem=packed_recv.at[part, i],
+            device_id={"grid": partner},
+            device_id_type=MESH,
+        )
+
+    for copy in tile_copies:
+        copy.wait()
+    for j in range(min(AHEAD, count)):
+        own_full(j, g >= 0)
+    for j in range(count):
+        own_trimmed(j)
     pool_copies = []
     for part in range(2):
-        for a in range(rows.shape[1]):
+        for a in range(total_blocks):
             copy = pltpu.make_async_copy(
                 pool.at[0, part, :, pl.ds(a * width, width)], rows.at[part, a], pool_sem.at[part, a]
             )
             copy.start()
             pool_copies.append(copy)
-    for distance in range(1, grid_size - 1):
-        for j in range(len(chunks)):
-            pass_on(j, distance)
+
+    def place_of(k, block):
+        hits = jnp.int32(0)
+        position = jnp.int32(0)
+        for n in range(listed_count):
+            hit = (ancestors[k, n] == block).astype(jnp.int32)
+            hits = hits + hit
+            position = position + hit * n
+        return hits, jnp.clip(position, 0, listed_count - 1)
+
+    @pl.when(is_end)
+    def _():
+        for j in range(count):
+            factors[j][:, pl.ds(shift_first, SHIFTED), :] = jnp.zeros(
+                (listed_count, SHIFTED, 2 * half), jnp.bfloat16
+            )
+
+    @pl.when(is_mid)
+    def _():
+        for copy in shifted_copies():
+            copy.wait()
+
+        @pl.loop(0, supers * HALVES)
+        def _(s):
+            for b in range(total_blocks):
+                hits, position = place_of(s // HALVES, b)
+                keep = jnp.full((SHIFTED, 2 * half), hits, jnp.int32) > 0
+                spread[s, pl.ds(b * SHIFTED, SHIFTED), :] = jnp.where(
+                    keep, shifted_tiles[s, position].astype(jnp.float32), 0.0
+                ).astype(jnp.bfloat16)
+
     for copy in pool_copies:
         copy.wait()
     diag_copy.wait()
+
+    @pl.when(is_end)
+    def _():
+        offset = lax.rem(shift_first, LANES)
+        lanes = pl.ds(pl.multiple_of(shift_first - offset, LANES), LANES)
+        shape = (GROUP * LANES, GROUP * SHIFTED)
+        row = lax.broadcasted_iota(jnp.int32, shape, 0)
+        col = lax.broadcasted_iota(jnp.int32, shape, 1)
+        lane = lax.rem(row, LANES) - offset
+        target = (row // LANES) * SHIFTED + lane
+        chosen = jnp.logical_and(jnp.logical_and(lane >= 0, lane < SHIFTED), target == col)
+        select[...] = chosen.astype(jnp.float32).astype(jnp.bfloat16)
+
+        @pl.loop(0, 2 * blocks)
+        def _(s):
+            part = lax.rem(s, 2)
+            i = s // 2
+            span = pl.ds(pl.multiple_of(i * width, width), width)
+            for group in range(total_blocks // GROUP):
+                left = jnp.concatenate(
+                    [rows[part, group * GROUP + b, span, lanes] for b in range(GROUP)], axis=1
+                )
+                packed[part, i, :, pl.ds(group * GROUP * SHIFTED, GROUP * SHIFTED)] = jnp.dot(
+                    left, select[...], preferred_element_type=jnp.float32
+                ).astype(jnp.bfloat16)
+
+        packed_copy(0).start()
+
+    own_full(AHEAD, is_end)
+
+    @pl.when(is_end)
+    def _():
+        packed_copy(1).start()
+
+    def bring(j):
+        if j + AHEAD + 1 < count:
+            own_full(j + AHEAD + 1, is_end)
+        if j + 2 < 2 * blocks:
+            @pl.when(is_end)
+            def _():
+                packed_copy(j + 2).start()
+        if j + AHEAD < count:
+            own_full(j + AHEAD, is_mid)
+
+        def from_below():
+            hop(j, g - 1, True).wait_recv()
+            hop(j, g - 1, True).start()
+
+        def from_above():
+            hop(j, g + 1, False).wait_recv()
+            hop(j, g + 1, False).start()
+
+        @pl.when(g == 1)
+        def _():
+            from_above()
+            from_below()
+            hop(j, g + 2, False).wait_recv()
+            hop(j, g + 2, False).start()
+
+        @pl.when(g == 2)
+        def _():
+            from_below()
+            from_above()
+            hop(j, g - 2, True).wait_recv()
+            hop(j, g - 2, True).start()
+
+        @pl.when(g == 0)
+        def _():
+            hop(j, g + 1, False, True).wait_recv()
+            hop(j, g + 2, False).wait_recv()
+            hop(j, g + 3, False).wait_recv()
+
+        @pl.when(g == last)
+        def _():
+            hop(j, g - 1, True, True).wait_recv()
+            hop(j, g - 2, True).wait_recv()
+            hop(j, g - 3, True).wait_recv()
 
     w_real = weight[0, 0]
     w_imag = weight[0, 1]
@@ -222,6 +369,37 @@
             device_id_type=MESH,
         )
 
+    def aid_copy(k, i):
+        slot = lax.rem(q - k + pole_size, pole_size) - 1
+        return pltpu.make_async_remote_copy(
+            src_ref=aid_sent.at[k, i],
+            dst_ref=aid_got.at[slot, i],
+            send_sem=aid_send.at[k, i],
+            recv_sem=aid_recv.at[slot, i],
+            device_id={"pole": k},
+            device_id_type=MESH,
+        )
+
+    def return_copy(i):
+        return pltpu.make_async_remote_copy(
+            src_ref=returned.at[i],
+            dst_ref=returned.at[i],
+            send_sem=return_send.at[i],
+            recv_sem=return_recv.at[i],
+            device_id={"grid": partner},
+            device_id_type=MESH,
+        )
+
+    def rows_copy(j):
+        return pltpu.make_async_remote_copy(
+            src_ref=column_rows.at[j],
+            dst_ref=column_rows.at[j],
+            send_sem=rows_send.at[j],
+            recv_sem=rows_recv.at[j],
+            device_id={"grid": partner},
+            device_id_type=MESH,
+        )
+
     def share_copy(k, r):
         return pltpu.make_async_remote_copy(
             src_ref=sent_diag.at[k, pl.ds(r * share, share)],
@@ -232,15 +410,6 @@
             device_id_type=MESH,
         )
 
-    def place_of(k, block):
-        count = jnp.int32(0)
-        position = jnp.int32(0)
-        for n in range(listed_count):
-            hit = (ancestors[k, n] == block).astype(jnp.int32)
-            count = count + hit
-            position = position + hit * n
-        return count, jnp.clip(position, 0, listed_count - 1)
-
     def grid_copy(k):
         return pltpu.make_async_remote_copy(
             src_ref=grid_send.at[k],
@@ -268,6 +437,19 @@
             device_id={"pole": q}, device_id_type=MESH,
         )
 
+    def parts_of(with_real, with_imag, hits):
+        keep = jnp.full((with_real.shape[0], half), hits, jnp.int32) > 0
+        real = jnp.where(keep, with_imag[:, half:] - with_real[:, :half], 0.0)
+        imag = jnp.where(keep, -(with_real[:, half:] + with_imag[:, :half]), 0.0)
+        return real, imag
+
+    def to_shares(k):
+        sent_diag[k] = own_diag[k].astype(jnp.bfloat16)
+        for r in range(pole_size):
+            @pl.when(q != r)
+            def _():
+                share_copy(k, r).start()
+
     def to_owner(k):
         for r in range(pole_size):
             @pl.when(q != r)
@@ -286,8 +468,61 @@
         def _():
             grid_sums[g] = grid_send[k]
 
+    def diag_terms(k, first_block, column_of, added):
+        for left in range(HALVES):
+            for right in range(HALVES):
+                total = jnp.zeros((2 * half, 2 * half), jnp.float32)
+                for b in range(blocks):
+                    _, position = place_of(k, first_block + b)
+                    total = total + lax.dot_general(
+                        factors[chunks.index((k, left))][position],
+                        column_of(b, right),
+                        (((0,), (0,)), ((), ())),
+                        preferred_element_type=jnp.float32,
+                    )
+                real = total[half:, half:] - total[:half, :half]
+                imag = -(total[:half, half:] + total[half:, :half])
+                place = (k, pl.ds(left * half, half), pl.ds(right * half, half))
+                term = w_real * imag + w_imag * real
+                own_diag[place] = own_diag[place] + term if added else term
+
+    def aid_product(i):
+        for part in range(2):
+            packed_copy(2 * i + part).wait_recv()
+
+        @pl.loop(0, supers * HALVES)
+        def _(s):
+            k = s // HALVES
+            factor = spread[s]
+            with_real = jnp.dot(packed[0, i], factor, preferred_element_type=jnp.float32)
+            with_imag = jnp.dot(packed[1, i], factor, preferred_element_type=jnp.float32)
+            hits, _ = place_of(k, partner * blocks + i)
+            real, imag = parts_of(with_real, with_imag, hits)
+            aid_column[s, i, :, pl.ds(0, half)] = real.astype(jnp.bfloat16)
+            aid_column[s, i, :, pl.ds(half, half)] = imag.astype(jnp.bfloat16)
+            term = w_real * imag + w_imag * real
+            lanes = pl.ds(pl.multiple_of(lax.rem(s, HALVES) * half, half), half)
+            aid_sent[k, i, :, lanes] = term.astype(jnp.bfloat16)
+
+            @pl.when(q == k)
+            def _():
+                aid_own[i, :, lanes] = term
+
+        for k in range(supers):
+            @pl.when(q != k)
+            def _():
+                aid_copy(k, i).start()
+
+    def aid_return(i):
+        total = aid_own[i]
+        for slot in range(pole_size - 1):
+            landing(aid_got.at[slot, i], aid_recv.at[slot, i]).wait_recv()
+            total = total + aid_got[slot, i].astype(jnp.float32)
+        returned[i] = total.astype(jnp.bfloat16)
+        return_copy(i).start()
+
     for j, (k, c) in enumerate(chunks):
-        pass_on(j, grid_size - 1)
+        bring(j)
 
         @pl.loop(0, blocks)
         def _(b):
@@ -295,23 +530,26 @@
             with_real = jnp.zeros((width, 2 * half), jnp.float32)
             with_imag = jnp.zeros((width, 2 * half), jnp.float32)
             for n in range(listed_count):
-                source = jnp.clip(ancestors[k, n], 0, rows.shape[1] - 1)
-                factor = factors[k][c, n]
+                source = jnp.clip(ancestors[k, n], 0, total_blocks - 1)
+                factor = factors[j][n]
                 with_real += jnp.dot(
                     rows[0, source, span, :], factor, preferred_element_type=jnp.float32
                 )
                 with_imag += jnp.dot(
                     rows[1, source, span, :], factor, preferred_element_type=jnp.float32
                 )
-            count, _ = place_of(k, g * blocks + b)
-            keep = jnp.full((width, half), count, jnp.int32) > 0
-            real = jnp.where(keep, with_imag[:, half:] - with_real[:, :half], 0.0)
-            imag = jnp.where(keep, -(with_real[:, half:] + with_imag[:, :half]), 0.0)
+            hits, _ = place_of(k, g * blocks + b)
+            real, imag = parts_of(with_real, with_imag, hits)
             column[span, pl.ds(c * 2 * half, half)] = real.astype(jnp.bfloat16)
             column[span, pl.ds(c * 2 * half + half, half)] = imag.astype(jnp.bfloat16)
             term = w_real * imag + w_imag * real
             sent_panel[k, c, span, :] = term.astype(jnp.bfloat16)
 
+            @pl.when(is_end)
+            def _():
+                first = pl.multiple_of(b * width + shift_first, 16)
+                column_rows[j, b] = column[pl.ds(first, SHIFTED), pl.ds(c * 2 * half, 2 * half)]
+
             @pl.when(q == k)
             def _():
                 panel_out[span, pl.ds(c * half, half)] = term
@@ -320,27 +558,16 @@
             def _():
                 panel_copy(j, k, c, b).start()
 
+        @pl.when(is_end)
+        def _():
+            rows_copy(j).start()
+
         if c == HALVES - 1:
-            for left in range(HALVES):
-                for right in range(HALVES):
-                    def add(b, total):
-                        _, position = place_of(k, g * blocks + b)
-                        span = pl.ds(pl.multiple_of(b * width, width), width)
-                        return total + lax.dot_general(
-                            factors[k][left, position],
-                            column[span, pl.ds(right * 2 * half, 2 * half)],
-                            (((0,), (0,)), ((), ())),
-                            preferred_element_type=jnp.float32,
-                        )
-
-                    total = jnp.zeros((2 * half, 2 * half), jnp.float32)
-                    for b in range(blocks):
-                        total = add(b, total)
-                    real = total[half:, half:] - total[:half, :half]
-                    imag = -(total[:half, half:] + total[half:, :half])
-                    own_diag[k, pl.ds(left * half, half), pl.ds(right * half, half)] = (
-                        w_real * imag + w_imag * real
-                    )
+            diag_terms(
+                k, g * blocks,
+                lambda b, right: column[pl.ds(b * width, width), pl.ds(right * 2 * half, 2 * half)],
+                False,
+            )
 
             @pl.when(g == k)
             def _():
@@ -350,16 +577,49 @@
                     + w_imag * diag_local[0].astype(jnp.float32)
                 )
 
-            sent_diag[k] = own_diag[k].astype(jnp.bfloat16)
-            for r in range(pole_size):
-                @pl.when(q != r)
+            @pl.when(is_end)
+            def _():
+                to_shares(k)
+                if j + 1 > HALVES:
+                    to_owner(chunks[j - HALVES][0])
+
+        for i, step in enumerate(AID_STEPS):
+            if step == j:
+                @pl.when(is_mid)
                 def _():
-                    share_copy(k, r).start()
-
-            if k:
-                to_owner(k - 1)
-
-    to_owner(supers - 1)
+                    aid_product(i)
+        for i, step in enumerate(RETURN_STEPS):
+            if step == j:
+                @pl.when(is_mid)
+                def _():
+                    aid_return(i)
+
+    @pl.when(is_mid)
+    def _():
+        for i in range(blocks):
+            if AID_STEPS[i] >= count:
+                aid_product(i)
+        for i in range(blocks):
+            if RETURN_STEPS[i] >= count:
+                aid_return(i)
+        for turn, k in enumerate(order):
+            for c in range(HALVES):
+                j = chunks.index((k, c))
+                s = k * HALVES + c
+                rows_copy(j).wait_recv()
+                for i in range(blocks):
+                    place = (s, i, pl.ds(shift_first, SHIFTED), slice(None))
+                    aid_column[place] = (
+                        aid_column[place].astype(jnp.float32) + column_rows[j, i].astype(jnp.float32)
+                    ).astype(jnp.bfloat16)
+            diag_terms(
+                k, partner * blocks, lambda b, right: aid_column[k * HALVES + right, b], True
+            )
+            to_shares(k)
+            if turn:
+                to_owner(order[turn - 1])
+
+    to_owner(order[-1])
     for s in range(grid_size):
         @pl.when(g != s)
         def _():
@@ -385,21 +645,58 @@
                 total = total + got_panel[slot, c, span, :].astype(jnp.float32)
             panel_out[span, lanes] = total
 
+    @pl.when(is_end)
+    def _():
+        for i in range(blocks):
+            return_copy(i).wait_recv()
+            span = pl.ds(i * width, width)
+            panel_out[span, :] = panel_out[span, :] + returned[i].astype(jnp.float32)
+
     for r in range(pole_size):
         @pl.when(q != r)
         def _():
             landing(final.at[pl.ds(r * share, share)], c_recv.at[r]).wait_recv()
     diag_out[...] = final[...]
 
-    for distance in range(grid_size - 1):
-        for j in range(len(chunks)):
-            @pl.when(jnp.logical_and(g - distance >= 0, g + 1 < grid_size))
-            def _():
-                hop(j, g - distance, True).wait_send()
-
-            @pl.when(jnp.logical_and(g + distance < grid_size, g >= 1))
-            def _():
-                hop(j, g + distance, False).wait_send()
+    for j in range(count):
+        @pl.when(g <= 1)
+        def _():
+            hop(j, g, True).wait_send()
+
+        @pl.when(g >= 2)
+        def _():
+            hop(j, g, False).wait_send()
+
+        @pl.when(g == 1)
+        def _():
+            hop(j, g, False, True).wait_send()
+            hop(j, g + 1, False).wait_send()
+            hop(j, g - 1, True).wait_send()
+            hop(j, g + 2, False).wait_send()
+
+        @pl.when(g == 2)
+        def _():
+            hop(j, g, True, True).wait_send()
+            hop(j, g - 1, True).wait_send()
+            hop(j, g + 1, False).wait_send()
+            hop(j, g - 2, True).wait_send()
+
+    @pl.when(is_end)
+    def _():
+        for p in range(2 * blocks):
+            packed_copy(p).wait_send()
+        for j in range(count):
+            rows_copy(j).wait_send()
+
+    @pl.when(is_mid)
+    def _():
+        for i in range(blocks):
+            return_copy(i).wait_send()
+            for k in range(supers):
+                @pl.when(q != k)
+                def _():
+                    aid_copy(k, i).wait_send()
+
     for j, (k, c) in enumerate(chunks):
         for b in range(blocks):
             @pl.when(q != k)
@@ -428,11 +725,12 @@
     share = width // pole_size
     chunks = supers * HALVES
     blocks = height // width
+    total_blocks = inverse_pool.shape[3] // width
     dma = pltpu.SemaphoreType.DMA
     f32 = jnp.float32
     bf16 = jnp.bfloat16
     scratch = [
-        pltpu.VMEM((2, inverse_pool.shape[3] // width, height, width), bf16),
+        pltpu.VMEM((2, total_blocks, height, width), bf16),
         pltpu.VMEM((supers, HALVES, height, half), bf16),
         pltpu.VMEM((pole_size - 1, HALVES, height, half), bf16),
         pltpu.VMEM((height, 2 * width), bf16),
@@ -443,13 +741,27 @@
         pltpu.VMEM((supers, share, width), f32),
         pltpu.VMEM((grid_size, share, width), f32),
         pltpu.VMEM((width, width), f32),
-        dma((2, inverse_pool.shape[3] // width)), dma((chunks, 2)), dma(()),
+        pltpu.VMEM((GROUP * LANES, GROUP * SHIFTED), bf16),
+        pltpu.VMEM((2, blocks, width, total_blocks * SHIFTED), bf16),
+        pltpu.VMEM((chunks, listed_count, SHIFTED, 2 * half), bf16),
+        pltpu.VMEM((chunks, total_blocks * SHIFTED, 2 * half), bf16),
+        pltpu.VMEM((chunks, blocks, width, 2 * half), bf16),
+        pltpu.VMEM((supers, blocks, width, width), bf16),
+        pltpu.VMEM((pole_size - 1, blocks, width, width), bf16),
+        pltpu.VMEM((blocks, width, width), f32),
+        pltpu.VMEM((blocks, width, width), bf16),
+        pltpu.VMEM((chunks, blocks, SHIFTED, 2 * half), bf16),
+        dma((2, total_blocks)), dma((chunks, 2)), dma(()), dma((supers, HALVES, 2)),
         dma((chunks, grid_size)), dma((chunks, grid_size)), dma((chunks, grid_size)),
         dma((chunks, blocks)), dma((pole_size - 1, HALVES, blocks)),
         dma((supers, pole_size)), dma((supers, pole_size)),
         dma((supers,)), dma((grid_size,)),
         dma((pole_size,)), dma((pole_size,)),
-    ] + [pltpu.VMEM((HALVES, listed_count, width, 2 * half), bf16)] * supers
+        dma((2, blocks)), dma((2, blocks)),
+        dma((supers, blocks)), dma((pole_size - 1, blocks)),
+        dma((blocks,)), dma((blocks,)),
+        dma((chunks,)), dma((chunks,)),
+    ] + [pltpu.VMEM((listed_count, width, 2 * half), bf16)] * chunks
     smem = pl.BlockSpec(memory_space=pltpu.SMEM)
     vmem = pl.BlockSpec(memory_space=pltpu.VMEM)
     anywhere = pl.BlockSpec(memory_space=pl.ANY)
@@ -463,7 +775,7 @@
         out_specs=(vmem, vmem),
         scratch_shapes=scratch,
         compiler_params=pltpu.CompilerParams(
-            collective_id=0, has_side_effects=True, vmem_limit_bytes=56 * 2**20
+            collective_id=0, has_side_effects=True, vmem_limit_bytes=60 * 2**20
         ),
     )(ancestors, pole_weight, inverse_pool, factor_tiles, diag_inverse)
 
@@ -472,7 +784,15 @@
     supers = ancestors.shape[0]
     width = factor_tiles.shape[5]
     whole_blocks = inverse_pool.shape[2] % width == 0 and factor_tiles.shape[4] % 16 == 0
-    if whole_blocks and supers == grid_size == pole_size and width % (HALVES * 128) == 0:
+    slice_rows = factor_tiles.shape[4]
+    suited = (
+        grid_size == 4
+        and LANES % slice_rows == 0
+        and SHIFTED < slice_rows
+        and (inverse_pool.shape[3] // width) % GROUP == 0
+        and inverse_pool.shape[2] == inverse_pool.shape[3] // grid_size
+    )
+    if whole_blocks and suited and supers == grid_size == pole_size and width == HALVES * LANES:
         return fused(
             grid_size, pole_size, inverse_pool, factor_tiles, diag_inverse, pole_weight, ancestors
         )

time: 201 us -> 193 us (0.960)
  the two profiles are of different devices: /device:TPU:29 before, /device:TPU:9 now
where the time goes in v2:
time: 193 us
  Pallas kernels  188 us (97%)
  local copies, waits for them, and re-layouts  3.93 us (2%)
    pallas_call x1, Pallas kernels, fused(): pl.pallas_call(functools.partial(fused_kernel, grid_size, pole_size), out...  188 us
    unnamed x2, local copies, waits for them, and re-layouts  3.93 us

profile of v2, /device:TPU:9, one launch (start us, length us, event | category | flops | bytes accessed | tf_op | source)
XLA Modules:
  0.0 192.9 jit_solution(12326006232946473412)
XLA Ops:
  0.6 188.3 %shard_map.68 = (f32[1024,256]{1,0:T(8,128)}, f32[256,256]{1,0:T(8,128)}) custom-call(s32[4,10]{1,0:T(4,128)} %ancestors.1, f32[1,2]{1,0:T(1,128)} %weight.1, bf16[1,2,1024,4096]{3,2,1,0:T(8,128)(2,1)} %pool.1, bf16[1,4,2,10,64,256]{5,4,3,2,1,0:T(8,128)(2,1)} %tiles.1, bf16[1,2,256,256]{3,2,1,0:T(8,128)(2,1)} %diag_in.1), custom_call_target="tpu_custom_call" | custom-call | tf_op jit(solution)/shard_map/pallas_call | solution.py:768
  188.9 2.3 %copy.9 = f32[1024,256]{1,0:T(8,128)} copy(f32[1024,256]{1,0:T(8,128)} %get-tuple-element.4) | data formatting | bytes 2097152
  191.2 1.7 copy.10

commit v3 on v2

--- a/solution.py
+++ b/solution.py
@@ -10,11 +10,14 @@
 MESH = pl.DeviceIdType.MESH
 HALVES = 2
 AHEAD = 2
+OWN_AHEAD = 3
+NEAR_AHEAD = 2
+EDGE_AHEAD = 1
 SHIFTED = 48
 LANES = 128
 GROUP = 8
-AID_STEPS = (3, 5, 7, 8)
-RETURN_STEPS = (4, 6, 8, 8)
+AID_STEPS = (2, 4, 6, 8)
+RETURN_STEPS = (3, 5, 7, 8)
 
 
 def plain_product(left, right):
@@ -230,8 +233,10 @@
 
     for copy in tile_copies:
         copy.wait()
-    for j in range(min(AHEAD, count)):
+    for j in range(AHEAD):
         own_full(j, g >= 0)
+    for j in range(AHEAD, OWN_AHEAD):
+        own_full(j, is_mid)
     for j in range(count):
         own_trimmed(j)
     pool_copies = []
@@ -302,43 +307,40 @@
                     left, select[...], preferred_element_type=jnp.float32
                 ).astype(jnp.bfloat16)
 
-        packed_copy(0).start()
-
-    own_full(AHEAD, is_end)
-
-    @pl.when(is_end)
-    def _():
-        packed_copy(1).start()
+        for p in range(2 * blocks):
+            packed_copy(p).start()
+            if AHEAD + p < count:
+                own_full(AHEAD + p, g >= 0)
 
     def bring(j):
-        if j + AHEAD + 1 < count:
-            own_full(j + AHEAD + 1, is_end)
-        if j + 2 < 2 * blocks:
-            @pl.when(is_end)
-            def _():
-                packed_copy(j + 2).start()
-        if j + AHEAD < count:
-            own_full(j + AHEAD, is_mid)
-
-        def from_below():
-            hop(j, g - 1, True).wait_recv()
-            hop(j, g - 1, True).start()
-
-        def from_above():
-            hop(j, g + 1, False).wait_recv()
-            hop(j, g + 1, False).start()
+        if j + OWN_AHEAD < count:
+            own_full(j + OWN_AHEAD, is_mid)
+        near = range(NEAR_AHEAD + 1) if j == 0 else range(j + NEAR_AHEAD, min(j + NEAR_AHEAD + 1, count))
+        edge = range(EDGE_AHEAD + 1) if j == 0 else range(j + EDGE_AHEAD, min(j + EDGE_AHEAD + 1, count))
+
+        def from_below(i):
+            hop(i, g - 1, True).wait_recv()
+            hop(i, g - 1, True).start()
+
+        def from_above(i):
+            hop(i, g + 1, False).wait_recv()
+            hop(i, g + 1, False).start()
 
         @pl.when(g == 1)
         def _():
-            from_above()
-            from_below()
+            for i in near:
+                from_above(i)
+            for i in edge:
+                from_below(i)
             hop(j, g + 2, False).wait_recv()
             hop(j, g + 2, False).start()
 
         @pl.when(g == 2)
         def _():
-            from_below()
-            from_above()
+            for i in near:
+                from_below(i)
+            for i in edge:
+                from_above(i)
             hop(j, g - 2, True).wait_recv()
             hop(j, g - 2, True).start()
 

time: 193 us -> 169 us (0.88)
  Pallas kernels: 188 us -> 164 us
    pallas_call x1, Pallas kernels: 188 us -> 164 us  [fused(): pl.pallas_call(functools.partial(fused_kernel, grid_size, pole_size), out...]
where the time goes in v3:
time: 169 us
  Pallas kernels  164 us (97%)
  local copies, waits for them, and re-layouts  3.93 us (2%)
    pallas_call x1, Pallas kernels, fused(): pl.pallas_call(functools.partial(fused_kernel, grid_size, pole_size), out...  164 us
    unnamed x2, local copies, waits for them, and re-layouts  3.93 us

profile of v3, /device:TPU:9, one launch (start us, length us, event | category | flops | bytes accessed | tf_op | source)
XLA Modules:
  0.0 168.9 jit_solution(12712552241892586906)
XLA Ops:
  0.6 164.4 %shard_map.68 = (f32[1024,256]{1,0:T(8,128)}, f32[256,256]{1,0:T(8,128)}) custom-call(s32[4,10]{1,0:T(4,128)} %ancestors.1, f32[1,2]{1,0:T(1,128)} %weight.1, bf16[1,2,1024,4096]{3,2,1,0:T(8,128)(2,1)} %pool.1, bf16[1,4,2,10,64,256]{5,4,3,2,1,0:T(8,128)(2,1)} %tiles.1, bf16[1,2,256,256]{3,2,1,0:T(8,128)(2,1)} %diag_in.1), custom_call_target="tpu_custom_call" | custom-call | tf_op jit(solution)/shard_map/pallas_call | solution.py:770
  165.0 2.3 %copy.9 = f32[1024,256]{1,0:T(8,128)} copy(f32[1024,256]{1,0:T(8,128)} %get-tuple-element.4) | data formatting | bytes 2097152
  167.3 1.7 copy.10

commit v4 on v3

--- a/solution.py
+++ b/solution.py
@@ -17,7 +17,10 @@
 LANES = 128
 GROUP = 8
 AID_STEPS = (2, 4, 6, 8)
-RETURN_STEPS = (3, 5, 7, 8)
+END_ORDER = (
+    ("packed", 0), ("own", 2), ("packed", 1), ("own", 3), ("own", 4), ("packed", 2), ("own", 5), ("packed", 3),
+    ("own", 6), ("packed", 4), ("own", 7), ("packed", 5), ("packed", 6), ("packed", 7),
+)
 
 
 def plain_product(left, right):
@@ -124,11 +127,11 @@
 def fused_kernel(
     grid_size, pole_size, ancestors, weight, pool, tiles, diag_in,
     panel_out, diag_out,
-    rows, sent_panel, got_panel, column, own_diag, sent_diag, diag_local, pole_sums, grid_send, grid_sums, final,
-    select, packed, shifted_tiles, spread, aid_column, aid_sent, aid_got, aid_own, returned, column_rows,
+    rows, sent_panel, got_panel, column, own_diag, diag_local, pole_sums, grid_send, grid_sums, own_sum, final,
+    select, packed, shifted_tiles, spread, aid_column, aid_sent, aid_got, aid_own, returned, column_rows, lent,
     pool_sem, tile_sem, diag_sem, shifted_sem, up_sem, down_sem, arrive_sem,
     panel_send, panel_recv, a_send, a_recv, b_send, b_recv, c_send, c_recv,
-    packed_send, packed_recv, aid_send, aid_recv, return_send, return_recv, rows_send, rows_recv, *factors,
+    packed_send, packed_recv, aid_send, aid_recv, return_send, return_recv, rows_send, rows_recv, lent_send, lent_recv, *factors,
 ):
     g = lax.axis_index("grid")
     q = lax.axis_index("pole")
@@ -278,6 +281,11 @@
                     keep, shifted_tiles[s, position].astype(jnp.float32), 0.0
                 ).astype(jnp.bfloat16)
 
+        for c in range(HALVES):
+            for b in range(blocks):
+                _, position = place_of(order[-1], partner * blocks + b)
+                lent[c, b] = shifted_tiles[order[-1] * HALVES + c, position]
+
     for copy in pool_copies:
         copy.wait()
     diag_copy.wait()
@@ -307,10 +315,11 @@
                     left, select[...], preferred_element_type=jnp.float32
                 ).astype(jnp.bfloat16)
 
-        for p in range(2 * blocks):
-            packed_copy(p).start()
-            if AHEAD + p < count:
-                own_full(AHEAD + p, g >= 0)
+        for name, index in END_ORDER:
+            if name == "packed":
+                packed_copy(index).start()
+            else:
+                own_full(index, g >= 0)
 
     def bring(j):
         if j + OWN_AHEAD < count:
@@ -392,19 +401,29 @@
             device_id_type=MESH,
         )
 
-    def rows_copy(j):
-        return pltpu.make_async_remote_copy(
-            src_ref=column_rows.at[j],
-            dst_ref=column_rows.at[j],
-            send_sem=rows_send.at[j],
-            recv_sem=rows_recv.at[j],
+    def lent_copy():
+        return pltpu.make_async_remote_copy(
+            src_ref=lent,
+            dst_ref=lent,
+            send_sem=lent_send,
+            recv_sem=lent_recv,
             device_id={"grid": partner},
             device_id_type=MESH,
         )
 
+    def rows_copy(j, b):
+        return pltpu.make_async_remote_copy(
+            src_ref=column_rows.at[j, b],
+            dst_ref=column_rows.at[j, b],
+            send_sem=rows_send.at[j, b],
+            recv_sem=rows_recv.at[j, b],
+            device_id={"grid": partner},
+            device_id_type=MESH,
+        )
+
     def share_copy(k, r):
         return pltpu.make_async_remote_copy(
-            src_ref=sent_diag.at[k, pl.ds(r * share, share)],
+            src_ref=own_diag.at[k, pl.ds(r * share, share)],
             dst_ref=pole_sums.at[k, q],
             send_sem=a_send.at[k, r],
             recv_sem=a_recv.at[k, q],
@@ -446,7 +465,6 @@
         return real, imag
 
     def to_shares(k):
-        sent_diag[k] = own_diag[k].astype(jnp.bfloat16)
         for r in range(pole_size):
             @pl.when(q != r)
             def _():
@@ -459,8 +477,8 @@
                 landing(pole_sums.at[k, r], a_recv.at[k, r]).wait_recv()
         summed = own_diag[k, pl.ds(pl.multiple_of(q * share, share), share), :]
         for step in range(1, pole_size):
-            summed = summed + pole_sums[k, lax.rem(q + step, pole_size)].astype(jnp.float32)
-        grid_send[k] = summed
+            summed = summed + pole_sums[k, lax.rem(q + step, pole_size)]
+        grid_send[k] = summed.astype(jnp.bfloat16)
 
         @pl.when(g != k)
         def _():
@@ -468,13 +486,20 @@
 
         @pl.when(g == k)
         def _():
-            grid_sums[g] = grid_send[k]
-
-    def diag_terms(k, first_block, column_of, added):
+            own_sum[...] = summed
+
+    def add_diag(k, left, right, total, added):
+        real = total[half:, half:] - total[:half, :half]
+        imag = -(total[:half, half:] + total[half:, :half])
+        place = (k, pl.ds(left * half, half), pl.ds(right * half, half))
+        term = w_real * imag + w_imag * real
+        own_diag[place] = own_diag[place] + term if added else term
+
+    def diag_terms(k, first_block, column_of, added, chosen):
         for left in range(HALVES):
             for right in range(HALVES):
                 total = jnp.zeros((2 * half, 2 * half), jnp.float32)
-                for b in range(blocks):
+                for b in chosen:
                     _, position = place_of(k, first_block + b)
                     total = total + lax.dot_general(
                         factors[chunks.index((k, left))][position],
@@ -482,11 +507,33 @@
                         (((0,), (0,)), ((), ())),
                         preferred_element_type=jnp.float32,
                     )
-                real = total[half:, half:] - total[:half, :half]
-                imag = -(total[:half, half:] + total[half:, :half])
-                place = (k, pl.ds(left * half, half), pl.ds(right * half, half))
-                term = w_real * imag + w_imag * real
-                own_diag[place] = own_diag[place] + term if added else term
+                add_diag(k, left, right, total, added)
+
+    def tile_rows(k, left):
+        return jnp.concatenate(
+            [
+                factors[chunks.index((k, left))][
+                    place_of(k, partner * blocks + b)[1], pl.ds(shift_first, SHIFTED), :
+                ]
+                for b in range(blocks)
+            ],
+            axis=0,
+        )
+
+    def lent_rows(k, left):
+        return lent[left].reshape(blocks * SHIFTED, 2 * half)
+
+    def rows_terms_added(k, rows_of):
+        for left in range(HALVES):
+            stacked = rows_of(k, left)
+            for right in range(HALVES):
+                total = lax.dot_general(
+                    stacked,
+                    column_rows[chunks.index((k, right))].reshape(blocks * SHIFTED, 2 * half),
+                    (((0,), (0,)), ((), ())),
+                    preferred_element_type=jnp.float32,
+                )
+                add_diag(k, left, right, total, True)
 
     def aid_product(i):
         for part in range(2):
@@ -525,6 +572,10 @@
 
     for j, (k, c) in enumerate(chunks):
         bring(j)
+        if j == count - 1:
+            @pl.when(is_mid)
+            def _():
+                lent_copy().start()
 
         @pl.loop(0, blocks)
         def _(b):
@@ -551,24 +602,23 @@
             def _():
                 first = pl.multiple_of(b * width + shift_first, 16)
                 column_rows[j, b] = column[pl.ds(first, SHIFTED), pl.ds(c * 2 * half, 2 * half)]
+                if k != order[-1]:
+                    rows_copy(j, b).start()
 
             @pl.when(q == k)
             def _():
                 panel_out[span, pl.ds(c * half, half)] = term
 
-            @pl.when(q != k)
-            def _():
-                panel_copy(j, k, c, b).start()
-
-        @pl.when(is_end)
-        def _():
-            rows_copy(j).start()
+            if j < count - 1:
+                @pl.when(q != k)
+                def _():
+                    panel_copy(j, k, c, b).start()
 
         if c == HALVES - 1:
             diag_terms(
                 k, g * blocks,
                 lambda b, right: column[pl.ds(b * width, width), pl.ds(right * 2 * half, 2 * half)],
-                False,
+                False, range(blocks),
             )
 
             @pl.when(g == k)
@@ -581,8 +631,20 @@
 
             @pl.when(is_end)
             def _():
+                if j == count - 1:
+                    lent_copy().wait_recv()
+                    rows_terms_added(k, lent_rows)
                 to_shares(k)
-                if j + 1 > HALVES:
+
+            if j == count - 1:
+                for b in range(blocks):
+                    @pl.when(q != k)
+                    def _():
+                        panel_copy(j, k, c, b).start()
+
+            if j + 1 > HALVES:
+                @pl.when(is_end)
+                def _():
                     to_owner(chunks[j - HALVES][0])
 
         for i, step in enumerate(AID_STEPS):
@@ -590,46 +652,45 @@
                 @pl.when(is_mid)
                 def _():
                     aid_product(i)
-        for i, step in enumerate(RETURN_STEPS):
-            if step == j:
-                @pl.when(is_mid)
-                def _():
-                    aid_return(i)
 
     @pl.when(is_mid)
     def _():
-        for i in range(blocks):
-            if AID_STEPS[i] >= count:
-                aid_product(i)
-        for i in range(blocks):
-            if RETURN_STEPS[i] >= count:
-                aid_return(i)
-        for turn, k in enumerate(order):
+        def aid_diag(chosen):
+            for k in order:
+                diag_terms(
+                    k, partner * blocks, lambda b, right: aid_column[k * HALVES + right, b], True, chosen
+                )
+
+        early = [i for i in range(blocks) if AID_STEPS[i] < count]
+        late = [i for i in range(blocks) if AID_STEPS[i] >= count]
+        def add_rows(k):
             for c in range(HALVES):
-                j = chunks.index((k, c))
-                s = k * HALVES + c
-                rows_copy(j).wait_recv()
-                for i in range(blocks):
-                    place = (s, i, pl.ds(shift_first, SHIFTED), slice(None))
-                    aid_column[place] = (
-                        aid_column[place].astype(jnp.float32) + column_rows[j, i].astype(jnp.float32)
-                    ).astype(jnp.bfloat16)
-            diag_terms(
-                k, partner * blocks, lambda b, right: aid_column[k * HALVES + right, b], True
-            )
+                for b in range(blocks):
+                    rows_copy(chunks.index((k, c)), b).wait_recv()
+            rows_terms_added(k, tile_rows)
             to_shares(k)
-            if turn:
-                to_owner(order[turn - 1])
+
+        for i in early:
+            aid_return(i)
+        aid_diag(early)
+        for i in late:
+            aid_product(i)
+        aid_diag(late)
+        to_shares(order[-1])
+        for k in order[:-1]:
+            add_rows(k)
+        for i in late:
+            aid_return(i)
+        for k in order[:-1]:
+            to_owner(k)
 
     to_owner(order[-1])
     for s in range(grid_size):
         @pl.when(g != s)
         def _():
             landing(grid_sums.at[s], b_recv.at[s]).wait_recv()
-    summed = grid_sums[0]
-    for s in range(1, grid_size):
-        summed = summed + grid_sums[s]
-    final[pl.ds(pl.multiple_of(q * share, share), share), :] = summed
+            own_sum[...] = own_sum[...] + grid_sums[s].astype(jnp.float32)
+    final[pl.ds(pl.multiple_of(q * share, share), share), :] = own_sum[...]
     for r in range(pole_size):
         @pl.when(q != r)
         def _():
@@ -687,11 +748,13 @@
     def _():
         for p in range(2 * blocks):
             packed_copy(p).wait_send()
-        for j in range(count):
-            rows_copy(j).wait_send()
+        for j in range(count - HALVES):
+            for b in range(blocks):
+                rows_copy(j, b).wait_send()
 
     @pl.when(is_mid)
     def _():
+        lent_copy().wait_send()
         for i in range(blocks):
             return_copy(i).wait_send()
             for k in range(supers):
@@ -737,11 +800,11 @@
         pltpu.VMEM((pole_size - 1, HALVES, height, half), bf16),
         pltpu.VMEM((height, 2 * width), bf16),
         pltpu.VMEM((supers, width, width), f32),
-        pltpu.VMEM((supers, width, width), bf16),
         pltpu.VMEM(diag_inverse.shape[1:], bf16),
-        pltpu.VMEM((supers, pole_size, share, width), bf16),
-        pltpu.VMEM((supers, share, width), f32),
-        pltpu.VMEM((grid_size, share, width), f32),
+        pltpu.VMEM((supers, pole_size, share, width), f32),
+        pltpu.VMEM((supers, share, width), bf16),
+        pltpu.VMEM((grid_size, share, width), bf16),
+        pltpu.VMEM((share, width), f32),
         pltpu.VMEM((width, width), f32),
         pltpu.VMEM((GROUP * LANES, GROUP * SHIFTED), bf16),
         pltpu.VMEM((2, blocks, width, total_blocks * SHIFTED), bf16),
@@ -753,6 +816,7 @@
         pltpu.VMEM((blocks, width, width), f32),
         pltpu.VMEM((blocks, width, width), bf16),
         pltpu.VMEM((chunks, blocks, SHIFTED, 2 * half), bf16),
+        pltpu.VMEM((HALVES, blocks, SHIFTED, 2 * half), bf16),
         dma((2, total_blocks)), dma((chunks, 2)), dma(()), dma((supers, HALVES, 2)),
         dma((chunks, grid_size)), dma((chunks, grid_size)), dma((chunks, grid_size)),
         dma((chunks, blocks)), dma((pole_size - 1, HALVES, blocks)),
@@ -762,7 +826,7 @@
         dma((2, blocks)), dma((2, blocks)),
         dma((supers, blocks)), dma((pole_size - 1, blocks)),
         dma((blocks,)), dma((blocks,)),
-        dma((chunks,)), dma((chunks,)),
+        dma((chunks, blocks)), dma((chunks, blocks)), dma(()), dma(()),
     ] + [pltpu.VMEM((listed_count, width, 2 * half), bf16)] * chunks
     smem = pl.BlockSpec(memory_space=pltpu.SMEM)
     vmem = pl.BlockSpec(memory_space=pltpu.VMEM)

time: 169 us -> 167 us (0.988)
  Pallas kernels: 164 us -> 162 us
    pallas_call x1, Pallas kernels: 164 us -> 162 us  [fused(): pl.pallas_call(functools.partial(fused_kernel, grid_size, pole_size), out...]
where the time goes in v4:
time: 167 us
  Pallas kernels  162 us (97%)
  local copies, waits for them, and re-layouts  3.93 us (2%)
    pallas_call x1, Pallas kernels, fused(): pl.pallas_call(functools.partial(fused_kernel, grid_size, pole_size), out...  162 us
    unnamed x2, local copies, waits for them, and re-layouts  3.93 us

profile of v4, /device:TPU:9, one launch (start us, length us, event | category | flops | bytes accessed | tf_op | source)
XLA Modules:
  0.0 166.9 jit_solution(16843718809643941473)
XLA Ops:
  0.6 162.3 %shard_map.68 = (f32[1024,256]{1,0:T(8,128)}, f32[256,256]{1,0:T(8,128)}) custom-call(s32[4,10]{1,0:T(4,128)} %ancestors.1, f32[1,2]{1,0:T(1,128)} %weight.1, bf16[1,2,1024,4096]{3,2,1,0:T(8,128)(2,1)} %pool.1, bf16[1,4,2,10,64,256]{5,4,3,2,1,0:T(8,128)(2,1)} %tiles.1, bf16[1,2,256,256]{3,2,1,0:T(8,128)(2,1)} %diag_in.1), custom_call_target="tpu_custom_call" | custom-call | tf_op jit(solution)/shard_map/pallas_call | solution.py:834
  162.9 2.3 %copy.9 = f32[1024,256]{1,0:T(8,128)} copy(f32[1024,256]{1,0:T(8,128)} %get-tuple-element.4) | data formatting | bytes 2097152
  165.2 1.7 copy.10

commit v5 on v4

--- a/solution.py
+++ b/solution.py
@@ -126,12 +126,12 @@
 
 def fused_kernel(
     grid_size, pole_size, ancestors, weight, pool, tiles, diag_in,
-    panel_out, diag_out,
-    rows, sent_panel, got_panel, column, own_diag, diag_local, pole_sums, grid_send, grid_sums, own_sum, final,
+    panel_result, diag_out,
+    panel_out, rows, sent_panel, got_panel, column, own_diag, diag_local, pole_sums, grid_send, grid_sums, own_sum, final,
     select, packed, shifted_tiles, spread, aid_column, aid_sent, aid_got, aid_own, returned, column_rows, lent,
     pool_sem, tile_sem, diag_sem, shifted_sem, up_sem, down_sem, arrive_sem,
     panel_send, panel_recv, a_send, a_recv, b_send, b_recv, c_send, c_recv,
-    packed_send, packed_recv, aid_send, aid_recv, return_send, return_recv, rows_send, rows_recv, lent_send, lent_recv, *factors,
+    packed_send, packed_recv, aid_send, aid_recv, return_send, return_recv, rows_send, rows_recv, lent_send, lent_recv, store_sem, *factors,
 ):
     g = lax.axis_index("grid")
     q = lax.axis_index("pole")
@@ -715,6 +715,8 @@
             span = pl.ds(i * width, width)
             panel_out[span, :] = panel_out[span, :] + returned[i].astype(jnp.float32)
 
+    panel_store = pltpu.make_async_copy(panel_out, panel_result, store_sem)
+    panel_store.start()
     for r in range(pole_size):
         @pl.when(q != r)
         def _():
@@ -780,6 +782,7 @@
         @pl.when(q != r)
         def _():
             final_copy(r).wait_send()
+    panel_store.wait()
 
 
 def fused(grid_size, pole_size, inverse_pool, factor_tiles, diag_inverse, pole_weight, ancestors):
@@ -795,6 +798,7 @@
     f32 = jnp.float32
     bf16 = jnp.bfloat16
     scratch = [
+        pltpu.VMEM((height, width), f32),
         pltpu.VMEM((2, total_blocks, height, width), bf16),
         pltpu.VMEM((supers, HALVES, height, half), bf16),
         pltpu.VMEM((pole_size - 1, HALVES, height, half), bf16),
@@ -826,7 +830,7 @@
         dma((2, blocks)), dma((2, blocks)),
         dma((supers, blocks)), dma((pole_size - 1, blocks)),
         dma((blocks,)), dma((blocks,)),
-        dma((chunks, blocks)), dma((chunks, blocks)), dma(()), dma(()),
+        dma((chunks, blocks)), dma((chunks, blocks)), dma(()), dma(()), dma(()),
     ] + [pltpu.VMEM((listed_count, width, 2 * half), bf16)] * chunks
     smem = pl.BlockSpec(memory_space=pltpu.SMEM)
     vmem = pl.BlockSpec(memory_space=pltpu.VMEM)
@@ -838,7 +842,7 @@
             jax.ShapeDtypeStruct((width, width), f32),
         ),
         in_specs=[smem, smem, anywhere, anywhere, anywhere],
-        out_specs=(vmem, vmem),
+        out_specs=(anywhere, vmem),
         scratch_shapes=scratch,
         compiler_params=pltpu.CompilerParams(
             collective_id=0, has_side_effects=True, vmem_limit_bytes=60 * 2**20

time: 167 us -> 167 us (level)
  no operation moved by 1% of the time
where the time goes in v5:
time: 167 us
  Pallas kernels  162 us (97%)
  local copies, waits for them, and re-layouts  3.93 us (2%)
    pallas_call x1, Pallas kernels, fused(): pl.pallas_call(functools.partial(fused_kernel, grid_size, pole_size), out...  162 us
    unnamed x2, local copies, waits for them, and re-layouts  3.93 us

profile of v5, /device:TPU:9, one launch (start us, length us, event | category | flops | bytes accessed | tf_op | source)
XLA Modules:
  0.0 166.5 jit_solution(5463206236941206695)
XLA Ops:
  0.6 161.9 %shard_map.68 = (f32[1024,256]{1,0:T(8,128)}, f32[256,256]{1,0:T(8,128)}) custom-call(s32[4,10]{1,0:T(4,128)} %ancestors.1, f32[1,2]{1,0:T(1,128)} %weight.1, bf16[1,2,1024,4096]{3,2,1,0:T(8,128)(2,1)} %pool.1, bf16[1,4,2,10,64,256]{5,4,3,2,1,0:T(8,128)(2,1)} %tiles.1, bf16[1,2,256,256]{3,2,1,0:T(8,128)(2,1)} %diag_in.1), custom_call_target="tpu_custom_call" | custom-call | tf_op jit(solution)/shard_map/pallas_call | solution.py:838
  162.6 2.3 %copy.9 = f32[1024,256]{1,0:T(8,128)} copy(f32[1024,256]{1,0:T(8,128)} %get-tuple-element.4) | data formatting | bytes 2097152
  164.8 1.7 %copy.10 = f32[256,256]{1,0:T(8,128)} copy(f32[256,256]{1,0:T(8,128)} %get-tuple-element.5) | data formatting | bytes 524288
